TPU v7x, 32 devices: a whole 2x2x4 slice. The times are simulated.
32 devices in a mesh: section: 2 (over x), dp: 4 (over z), mp: 4 (over y, core).
Axes of the slice: x: 2, y: 2, z: 4, core: 2. Of those that a mesh axis runs over, the one named last changes fastest.
Arguments:
- hidden: bfloat16 [2, 512, 4096], P('section', 'dp'), may hold values from -9 to 9
- norm_gain: float32 [2, 4096], P('section'), may hold values from 0.5 to 1.5
- kv_weight: bfloat16 [2, 4096, 2048], P('section', None, 'mp'), may hold values from -1 to 1
- attn_flat: bfloat16 [2, 4, 8388608], P('section', 'mp', 'dp'), may hold values from -1 to 1
- final_gain: float32 [4096], replicated, may hold values from 0.5 to 1.5
- reward_head: float32 [4096], replicated, may hold values from -0.09375 to 0.09375
- segment_ids: int32 [2, 4], P('section'), may hold values from 0 to 2, never falling along the last dimension, each value on 1 to 2 neighbouring positions
- ranks: int32 [2], replicated, may hold values from 0 to 999
Outputs:
- next_hidden: bfloat16 [2, 512, 4096], P('section', 'dp')
- rewards: float32 [2], replicated
- pair_loss: float32 [2, 2], replicated
Inputs may be any that keep to these rules, and one draw needn't show every extreme that they name: `segment_ids`: each row's segment numbers never fall, every number of 0 to 2 is present, each on 1 to 2 blocks, one on exactly 2.
All inputs are finite; a program needn't handle non-finite values.
Results may differ from a plain program's by a relative error of at most 0.035.
Values may be sent and summed in bfloat16 or wider, within the bound.
A program may use at most 128 MiB of HBM per device.

v0:
```python
import jax
import jax.numpy as jnp
from jax import lax
from jax.sharding import PartitionSpec as P

HD = 128
QH = 32
KVH = 8
EPS = 1e-05


def passed_along(block, axis, distance):
    devices = range(lax.axis_size(axis))
    route = [(i - distance, i) for i in devices if i - distance in devices]
    return lax.ppermute(block, axis, route)


def shards(hidden, norm_gain, kv_weight, attn_flat, final_gain, reward_head, segment_ids, ranks):
    state = hidden[0]
    tokens = state.shape[0]
    width = state.shape[1]
    seg_row = segment_ids[0]
    blocks = lax.axis_size("dp")
    block = lax.axis_index("dp")
    phases = lax.axis_size("section")
    phase_now = lax.axis_index("section")
    responses = ranks.shape[0]
    state_wide = state.astype(jnp.float32)
    normed = (
        state_wide
        * lax.rsqrt(jnp.mean(state_wide * state_wide, -1, keepdims=True) + EPS)
        * norm_gain[0]
    ).astype(jnp.bfloat16)
    keyval = jnp.dot(normed, kv_weight[0], preferred_element_type=jnp.float32).astype(jnp.bfloat16)
    kv_local = keyval.shape[1] // (2 * HD)
    group = QH // KVH
    q_width = kv_local * group * HD
    flat = lax.all_gather(attn_flat[0, 0], "dp", axis=0, tiled=True)
    w_query = flat[: width * q_width].reshape(width, q_width)
    w_out = flat[width * q_width : 2 * width * q_width].reshape(q_width, width)
    query = jnp.dot(normed, w_query, preferred_element_type=jnp.float32).astype(jnp.bfloat16)
    query = query.reshape(tokens, kv_local, group, HD)
    block_ids = jnp.arange(blocks, dtype=jnp.int32)
    own_seg = jnp.sum(jnp.where(block_ids == block, seg_row, 0))
    query_pos = block * tokens + jnp.arange(tokens, dtype=jnp.int32)
    piece = lax.all_gather(keyval, "dp", axis=0, tiled=True)
    peak = jnp.full((kv_local, group, tokens), -1e30, jnp.float32)
    count = piece.shape[0]
    key_pos = jnp.arange(count, dtype=jnp.int32)
    key_block = key_pos // tokens
    key_seg = jnp.sum(jnp.where(key_block[:, None] == block_ids[None, :], seg_row[None, :], 0), 1)
    parts = piece.reshape(count, kv_local, 2, HD)
    keys = parts[:, :, 0]
    values = parts[:, :, 1]
    earlier = (key_block < block) & (key_block >= 0) & ((key_seg == 0) | (key_seg == own_seg))
    same = (key_block == block)[None, :] & (key_pos[None, :] <= query_pos[:, None])
    visible = earlier[None, :] | same
    scores = jnp.einsum("tjgd,cjd->jgtc", query, keys, preferred_element_type=jnp.float32) * HD ** (
        -0.5
    )
    scores = jnp.where(visible[None, None], scores, -1e30)
    new_peak = jnp.maximum(peak, jnp.max(scores, -1))
    weights = jnp.where(visible[None, None], jnp.exp(scores - new_peak[..., None]), 0.0)
    total = jnp.sum(weights, -1)
    accum = jnp.einsum(
        "jgtc,cjd->jgtd", weights.astype(jnp.bfloat16), values, preferred_element_type=jnp.float32
    )
    peak, total, accum = (new_peak, total, accum)
    mixed = (
        (accum / total[..., None])
        .transpose(2, 0, 1, 3)
        .reshape(tokens, q_width)
        .astype(jnp.bfloat16)
    )
    partial_value = jnp.dot(mixed, w_out, preferred_element_type=jnp.float32)
    ends = (
        jnp.sum(
            (seg_row[None, :] <= jnp.arange(1, responses + 1, dtype=jnp.int32)[:, None]).astype(
                jnp.int32
            ),
            1,
        )
        - 1
    )
    at_end = (ends == block) & (phase_now == phases - 1)
    summed = lax.psum(partial_value.astype(jnp.bfloat16), "mp").astype(jnp.float32)
    updated = (state_wide + summed).astype(jnp.bfloat16)
    moved = passed_along(updated, "section", 1)
    last_row = updated[tokens - 1].astype(jnp.float32)
    squares = jnp.sum(last_row * last_row)
    product = jnp.sum(last_row * final_gain * reward_head)
    sums_sq, dots = lax.psum(
        (jnp.where(at_end, squares, 0.0), jnp.where(at_end, product, 0.0)), ("section", "dp")
    )
    rewards = dots * lax.rsqrt(sums_sq / width + EPS)
    pair_loss = jnp.where(
        ranks[:, None] < ranks[None, :], jax.nn.softplus(rewards[None, :] - rewards[:, None]), 0.0
    )
    return (moved[None], rewards, pair_loss)


def solution(mesh):
    placed = (
        P("section", "dp", None),
        P("section", None),
        P("section", None, "mp"),
        P("section", "mp", "dp"),
        P(),
        P(),
        P("section", None),
        P(),
    )
    return jax.shard_map(
        shards,
        mesh=mesh,
        in_specs=placed,
        out_specs=(P("section", "dp", None), P(), P()),
        check_vma=False,
    )
```

profile of v0, /device:TPU:0, one launch (start us, length us, event | category | flops | bytes accessed | tf_op | source)
XLA Modules:
  0.0 864.1 jit_solution(7415746184136145379)
XLA Ops:
  7.2 0.0 copy-start.1
  7.2 0.0 copy-start.7
  7.2 0.0 all-gather.3.cloned.1.call-start
  7.2 0.7 all-gather.3.cloned.1.call-update
  7.9 0.0 all-reduce.3.cloned.1.call-start
  8.0 0.4 copy-done.1
  8.4 0.3 fusion.5
  8.7 0.0 copy-done.7
  8.7 2.9 fusion.16
  11.6 17.4 %all_gather.6 = bf16[512,512]{1,0:T(8,128)(2,1)S(1)} all-gather(bf16[128,512]{1,0:T(8,128)(2,1)S(1)} %fusion.16), channel_id=1, replica_groups=mesh['section'=2,'dp'=4,'mp'=4] {'dp'}, dimensions={0}, use_global_device_ids=true | all-gather | bytes 655360 | tf_op jit(solution)/shard_map/all_gather | solution.py:46
  29.0 0.0 copy-start.6
  29.0 0.1 reshape.161
  29.1 0.7 fusion.48
  29.9 0.7 copy.22
  30.6 0.0 copy-done.6
  30.6 0.6 fusion.44
  31.2 0.1 select_reduce_fusion
  31.3 0.7 or_and_fusion
  32.0 0.2 fusion.35
  32.2 541.5 %all-gather.3.cloned.1.call-done = bf16[1,1,8388608]{2,1,0:T(2,128)(2,1)} async-done(((bf16[1,1,2097152]{2,1,0:T(2,128)(2,1)}), bf16[1,1,8388608]{2,1,0:T(2,128)(2,1)}) %all-gather.3.cloned.1.call-update) | async-done | bytes 16777232 | tf_op jit(solution)/shard_map/all_gather | solution.py:38
  573.7 183.8 %slice_reduce_fusion = (bf16[4194304]{0:T(1024)(128)(2,1)}, bf16[4194304]{0:T(1024)(128)(2,1)}) fusion(bf16[1,1,8388608]{2,1,0:T(2,128)(2,1)} %all-gather.3.cloned.1.call-done), kind=kLoop, calls=%fused_computation | loop fusion | bytes 33554432 | tf_op jit(solution)/shard_map/slice | solution.py:40
  757.6 13.3 %slice.40 = bf16[1024,4096]{1,0:T(8,128)(2,1)} reshape(bf16[4194304]{0:T(1024)(128)(2,1)} %get-tuple-element.3) | data formatting | bytes 16777216 | tf_op jit(solution)/shard_map/slice | solution.py:40
  770.9 13.3 %slice.37 = bf16[4096,1024]{1,0:T(8,128)(2,1)} reshape(bf16[4194304]{0:T(1024)(128)(2,1)} %get-tuple-element.4) | data formatting | bytes 16777216 | tf_op jit(solution)/shard_map/slice | solution.py:39
  784.2 4.7 convolution_convert_fusion.1
  788.9 0.2 reshape.162
  789.0 0.0 copy-start
  789.0 0.5 fusion.11
  789.5 0.5 fusion.12
  790.1 0.7 fusion.15
  790.7 1.7 copy-done
  792.4 2.3 convolution_convert_fusion
  794.7 0.0 copy-start.2
  794.7 0.0 copy-start.3
  794.7 0.0 all-reduce.3.cloned.1.call-update
  794.7 0.2 fusion.43
  794.9 34.2 %all-reduce.3.cloned.1.call-done = bf16[128,4096]{1,0:T(8,128)(2,1)} async-done(((bf16[128,4096]{1,0:T(8,128)(2,1)}), bf16[128,4096]{1,0:T(8,128)(2,1)}) %all-reduce.3.cloned.1.call-update) | async-done | bytes 1048592 | tf_op jit(solution)/shard_map/psum | solution.py:86
  829.1 1.5 fusion.8
  830.6 3.4 collective-permute-start
  834.1 0.0 copy-done.2
  834.1 0.0 copy-done.3
  834.1 0.6 multiply_reduce_fusion
  834.7 1.3 broadcast_select_fusion
  836.0 19.5 %all-reduce = (f32[2]{0:T(128)S(1)}, f32[2]{0:T(128)S(1)}) all-reduce(f32[2]{0:T(128)S(1)} %get-tuple-element.12, f32[2]{0:T(128)S(1)} %get-tuple-element.11), channel_id=1, replica_groups=mesh['section'=2,'dp'=4,'mp'=4] {'section','dp'}, use_global_device_ids=true, to_apply=%region_8.9 | all-reduce | flops 4 | bytes 32 | tf_op jit(solution)/shard_map/psum | solution.py:92
  855.5 0.0 copy-done.4
  855.5 0.7 compare_select_fusion.1
  856.2 0.1 collective-permute-done
  856.3 1.0 copy.34
  857.3 0.0 copy-done.5
  (9 shorter events, 0.1 us)
Async XLA Ops:
  7.2 1.2 copy-start.1
  7.2 1.5 copy-start.7
  7.2 566.5 %all-gather.3.cloned.1.call-start = ((), (), s32[]{:S(2)}) async-start(), calls=%async_computation.1 | async-start | bytes 41943040 | tf_op jit(solution)/shard_map/all_gather | solution.py:38
  7.9 821.2 %all-reduce.3.cloned.1.call-start = ((), (), s32[]{:S(2)}) async-start(), calls=%async_computation | async-start | bytes 2097152 | tf_op jit(solution)/shard_map/psum | solution.py:86
  29.0 1.6 copy-start.6
  789.0 3.4 copy-start
  794.7 39.4 %copy-start.2 = (f32[4096]{0:T(1024)S(1)}, f32[4096]{0:T(1024)}, u32[]{:S(2)}) copy-start(f32[4096]{0:T(1024)} %param.13) | copy-start | bytes 49156
  794.7 39.4 %copy-start.3 = (f32[4096]{0:T(1024)S(1)}, f32[4096]{0:T(1024)}, u32[]{:S(2)}) copy-start(f32[4096]{0:T(1024)} %param.12) | copy-start | bytes 49156
  794.7 60.9 %copy-start.4 = (s32[2]{0:T(128)S(1)}, s32[2]{0:T(128)}, u32[]{:S(2)}) copy-start(s32[2]{0:T(128)} %param.15) | copy-start | bytes 28
  830.6 25.7 %collective-permute-start = (bf16[128,4096]{1,0:T(8,128)(2,1)S(1)}, bf16[128,4096]{1,0:T(8,128)(2,1)S(1)}, u32[]{:S(2)}, u32[]{:S(2)}) collective-permute-start(bf16[128,4096]{1,0:T(8,128)(2,1)S(1)} %fusion.8), channel_id=1, source_target_pairs={{0,16},{1,17},{2,18},{3,19},{4,20},{5,21},{6,22},{7,23},{8,24},{9,... | collective-permute-start | bytes 3145736 | tf_op jit(solution)/shard_map/ppermute | solution.py:15
  855.5 1.8 copy-start.5
Sparse Core Ops, SparseCore 0:
  9.6 564.0 all-gather.2
  794.8 34.2 all-reduce.2
where the time goes:
time: 865 us; the launch traced here: 864 us
  waiting for transfers between devices  577 us (67%)
  local copies, waits for them, and re-layouts  215 us (25%)
  blocking collectives  36.9 us (4%)
  between operations  14.3 us (2%)
  matrix products  11 us (1%)
    all_gather x1, waiting for transfers between devices, shards(): flat = lax.all_gather(attn_flat[0, 0], 'dp', axis=0, tiled=True)  542 us
    slice x2, local copies, waits for them, and re-layouts, shards(): w_out = flat[width * q_width:2 * width * q_width].reshape(q_width, width)  197 us
    psum x1, waiting for transfers between devices, shards(): lax.psum(partial_value.astype(jnp.bfloat16), 'mp').astype(jnp.float32)  34.2 us
    psum x1, blocking collectives, shards(): lax.psum((jnp.where(at_end, squares, 0.0), jnp.where(at_end, product, 0.0...  19.5 us
    all_gather x1, blocking collectives, shards(): piece = lax.all_gather(keyval, 'dp', axis=0, tiled=True)  17.4 us
  transfers between devices with their start and end apart: 3, of which 3 were waited for; matrix products, arithmetic and copies ran while one was open for 1% of the time, Pallas kernels for 0%

commit v1 on v0

--- a/solution.py
+++ b/solution.py
@@ -7,6 +7,18 @@
 QH = 32
 KVH = 8
 EPS = 1e-05
+
+
+def doubled_up(shard, axis, dim):
+    ways, here = (lax.axis_size(axis), lax.axis_index(axis))
+    grown, reach = (shard, 1)
+    while reach < ways:
+        theirs = lax.ppermute(grown, axis, [(d, d ^ reach) for d in range(ways)])
+        mine_first = jnp.concatenate([grown, theirs], axis=dim)
+        theirs_first = jnp.concatenate([theirs, grown], axis=dim)
+        grown = jnp.where(here & reach == 0, mine_first, theirs_first)
+        reach = 2 * reach
+    return grown
 
 
 def passed_along(block, axis, distance):
@@ -35,7 +47,7 @@
     kv_local = keyval.shape[1] // (2 * HD)
     group = QH // KVH
     q_width = kv_local * group * HD
-    flat = lax.all_gather(attn_flat[0, 0], "dp", axis=0, tiled=True)
+    flat = doubled_up(attn_flat[0, 0], "dp", 0)
     w_query = flat[: width * q_width].reshape(width, q_width)
     w_out = flat[width * q_width : 2 * width * q_width].reshape(q_width, width)
     query = jnp.dot(normed, w_query, preferred_element_type=jnp.float32).astype(jnp.bfloat16)

time: 865 us -> 735 us (0.85)
  waiting for transfers between devices: 577 us -> 125 us
  blocking collectives: 36.9 us -> 374 us
  local copies, waits for them, and re-layouts: 215 us -> 59.7 us
  other arithmetic: 6.63 us -> 127 us
  matrix products: 11 us -> 24.9 us
    all_gather x1 -> x0, waiting for transfers between devices: 542 us -> none  [shards(): flat = lax.all_gather(attn_flat[0, 0], 'dp', axis=0, tiled=True)]
    all_gather x1, blocking collectives: 17.4 us -> 354 us  [shards(): piece = lax.all_gather(keyval, 'dp', axis=0, tiled=True)]
    slice x3 -> x0, local copies, waits for them, and re-layouts: 210 us -> none  [the longest x2 197 us: shards(): w_out = flat[width * q_width:2 * width * q_width].reshape(q_width, width)]
    ppermute x0 -> x2, waiting for transfers between devices: none -> 90.9 us  [doubled_up(): theirs = lax.ppermute(grown, axis, [(d, d ^ reach) for d in range(ways)])]
    unnamed x0 -> x1, other arithmetic: none -> 90 us
    concatenate x0 -> x6, local copies, waits for them, and re-layouts: none -> 55.9 us  [doubled_up(): mine_first = jnp.concatenate([grown, theirs], axis=dim)]
    select_n x0 -> x3, other arithmetic: none -> 29.9 us  [doubled_up(): grown = jnp.where(here & reach == 0, mine_first, theirs_first)]
    dot_general x1, matrix products: 2.25 us -> 11.1 us  [shards(): partial_value = jnp.dot(mixed, w_out, preferred_element_type=jnp.float32)]
  transfers between devices with their start and end apart: 3 -> 4, of which waited for: 3 -> 3; matrix products, arithmetic and copies ran while one was open for 1% -> 8% of each run, Pallas kernels for 0% -> 0%
where the time goes in v1:
time: 735 us; the launch traced here: 734 us
  blocking collectives  374 us (51%)
  other arithmetic  127 us (17%)
  waiting for transfers between devices  125 us (17%)
  local copies, waits for them, and re-layouts  59.7 us (8%)
  matrix products  24.9 us (3%)
  between operations  14.2 us (2%)
  starting transfers between devices  9.32 us (1%)
    all_gather x1, blocking collectives, shards(): piece = lax.all_gather(keyval, 'dp', axis=0, tiled=True)  354 us
    ppermute x2, waiting for transfers between devices, doubled_up(): theirs = lax.ppermute(grown, axis, [(d, d ^ reach) for d in range(ways)])  90.9 us
    unnamed x1, other arithmetic  90 us
    concatenate x6, local copies, waits for them, and re-layouts, doubled_up(): mine_first = jnp.concatenate([grown, theirs], axis=dim)  55.9 us
    psum x1, waiting for transfers between devices, shards(): lax.psum(partial_value.astype(jnp.bfloat16), 'mp').astype(jnp.float32)  34.4 us
    select_n x3, other arithmetic, doubled_up(): grown = jnp.where(here & reach == 0, mine_first, theirs_first)  29.9 us
    psum x1, blocking collectives, shards(): lax.psum((jnp.where(at_end, squares, 0.0), jnp.where(at_end, product, 0.0...  19.5 us
  transfers between devices with their start and end apart: 4, of which 3 were waited for; matrix products, arithmetic and copies ran while one was open for 8% of the time, Pallas kernels for 0%

profile of v1, /device:TPU:0, one launch (start us, length us, event | category | flops | bytes accessed | tf_op | source)
XLA Modules:
  0.0 733.9 jit_solution(6778951180929668952)
XLA Ops:
  7.2 0.0 all-reduce.3.cloned.1.call-start
  7.2 90.0 %reduce = bf16[2097152]{0:T(1024)(128)(2,1)} reduce(bf16[1,1,2097152]{2,1,0:T(2,128)(2,1)} %param.11, bf16[]{:T(256)} %constant.65), dimensions={0,1}, to_apply=%param.11.reduce_sub_computation | reduce | bytes 8388610 | tf_op args[3]
  97.2 3.0 collective-permute-start
  100.3 90.9 %collective-permute-done = bf16[2097152]{0:T(1024)(128)(2,1)} collective-permute-done((bf16[2097152]{0:T(1024)(128)(2,1)}, bf16[2097152]{0:T(1024)(128)(2,1)}, u32[]{:S(2)}, u32[]{:S(2)}) %collective-permute-start) | collective-permute-done | bytes 4194336 | tf_op jit(solution)/shard_map/ppermute | solution.py:16
  191.2 13.0 %maximum_select_fusion.1 = bf16[4194304]{0:T(1024)(128)(2,1)} fusion(bf16[2097152]{0:T(1024)(128)(2,1)} %collective-permute-done, bf16[2097152]{0:T(1024)(128)(2,1)} %reduce, pred[]{:T(512)S(6)} %eq.69), kind=kLoop, calls=%fused_computation.10 | loop fusion | flops 37748736 | bytes 16777216 | tf_op jit(solution)/shard_map/jit(_where)/select_n | solution.py:19
  204.2 2.8 collective-permute-start.1
  207.0 7.3 concatenate.44
  214.3 7.3 concatenate.53
  221.7 0.0 copy-done.2
  221.7 0.3 fusion.18
  222.0 0.0 copy-done.8
  222.0 2.9 fusion.32
  224.9 354.4 %all_gather.3 = bf16[512,512]{1,0:T(8,128)(2,1)S(1)} all-gather(bf16[128,512]{1,0:T(8,128)(2,1)S(1)} %fusion.32), channel_id=1, replica_groups=mesh['section'=2,'dp'=4,'mp'=4] {'dp'}, dimensions={0}, use_global_device_ids=true | all-gather | bytes 655360 | tf_op jit(solution)/shard_map/all_gather | solution.py:58
  579.3 0.1 reshape.167
  579.4 0.7 fusion.66
  580.1 0.7 copy.22
  580.9 0.0 copy-done.7
  580.9 0.6 fusion.60
  581.5 0.1 select_reduce_fusion
  581.6 0.7 or_and_fusion
  582.2 0.2 fusion.51
  582.5 7.3 concatenate.45
  589.8 7.3 concatenate.54
  597.1 10.5 %maximum_select_fusion = bf16[4096,1024]{1,0:T(8,128)(2,1)} fusion(bf16[2048,1024]{1,0:T(8,128)(2,1)} %concatenate.45, bf16[2048,1024]{1,0:T(8,128)(2,1)} %concatenate.44, pred[]{:T(512)S(6)} %eq.69), kind=kLoop, calls=%fused_computation.9 | loop fusion | flops 37748736 | bytes 16777216 | tf_op jit(solution)/shard_map/jit(_where)/select_n | solution.py:19
  607.6 0.0 copy-done
  607.6 1.1 copy-done.1
  608.7 6.3 maximum_select_fusion.2
  615.0 0.0 collective-permute-done.1
  615.0 13.3 %concatenate.50 = bf16[4096,1024]{1,0:T(8,128)(2,1)} reshape(bf16[4194304]{0:T(1024)(128)(2,1)} %collective-permute-done.1) | data formatting | bytes 16777216 | tf_op jit(solution)/shard_map/concatenate | solution.py:17
  628.3 9.7 %fusion.29 = bf16[128,1024]{1,0:T(8,128)(2,1)S(1)} fusion(bf16[4096,1024]{1,0:T(8,128)(2,1)} %concatenate.50, bf16[4096,1024]{1,0:T(8,128)(2,1)} %maximum_select_fusion, pred[]{:T(512)S(6)} %eq.68, bf16[1,128,4096]{2,1,0:T(8,128)(2,1)S(1)} %copy-done.2, f32[4096]{0:T(1024)S(1)} %bitcast.70, f32[128]{0:T(128)S(1)} %add_rsqrt_fusion), kind=kOutput, calls=%fused_computation.37 | convolution fusion | flops 1113718784 | bytes 18104832 | tf_op jit(solution)/shard_map/dot_general | solution.py:53
  638.0 0.2 reshape.168
  638.2 0.5 fusion.24
  638.7 0.5 fusion.25
  639.2 0.7 fusion.28
  639.9 13.3 %concatenate.57 = bf16[1024,4096]{1,0:T(8,128)(2,1)} reshape(bf16[4194304]{0:T(1024)(128)(2,1)} %collective-permute-done.1) | data formatting | bytes 16777216 | tf_op jit(solution)/shard_map/concatenate | solution.py:17
  653.2 11.1 %fusion.10 = bf16[128,4096]{1,0:T(8,128)(2,1)} fusion(bf16[128,1024]{0,1:T(8,128)(2,1)S(1)} %bitcast.71, bf16[1024,4096]{1,0:T(8,128)(2,1)} %concatenate.57, bf16[1024,4096]{1,0:T(8,128)(2,1)} %maximum_select_fusion.2, pred[]{:T(512)S(6)} %eq.68), kind=kOutput, calls=%fused_computation.15 | convolution fusion | flops 1112014848 | bytes 18087936 | tf_op jit(solution)/shard_map/dot_general | solution.py:87
  664.3 0.0 all-reduce.3.cloned.1.call-update
  664.3 0.2 fusion.59
  664.5 34.4 %all-reduce.3.cloned.1.call-done = bf16[128,4096]{1,0:T(8,128)(2,1)} async-done(((bf16[128,4096]{1,0:T(8,128)(2,1)}), bf16[128,4096]{1,0:T(8,128)(2,1)}) %all-reduce.3.cloned.1.call-update) | async-done | bytes 1048592 | tf_op jit(solution)/shard_map/psum | solution.py:98
  698.9 1.5 fusion.21
  700.4 3.4 collective-permute-start.2
  703.9 0.0 copy-done.3
  703.9 0.6 multiply_reduce_fusion
  704.5 1.3 broadcast_select_fusion
  705.8 19.5 %all-reduce = (f32[2]{0:T(128)S(1)}, f32[2]{0:T(128)S(1)}) all-reduce(f32[2]{0:T(128)S(1)} %get-tuple-element.10, f32[2]{0:T(128)S(1)} %get-tuple-element.9), channel_id=1, replica_groups=mesh['section'=2,'dp'=4,'mp'=4] {'section','dp'}, use_global_device_ids=true, to_apply=%region_8.9 | all-reduce | flops 4 | bytes 32 | tf_op jit(solution)/shard_map/psum | solution.py:104
  725.3 0.7 compare_select_fusion.1
  726.0 0.1 collective-permute-done.2
  726.1 1.0 copy.34
  (19 shorter events, 0.1 us)
Async XLA Ops:
  7.2 691.7 %all-reduce.3.cloned.1.call-start = ((), (), s32[]{:S(2)}) async-start(), calls=%async_computation | async-start | bytes 2097152 | tf_op jit(solution)/shard_map/psum | solution.py:98
  97.2 93.9 %collective-permute-start = (bf16[2097152]{0:T(1024)(128)(2,1)}, bf16[2097152]{0:T(1024)(128)(2,1)}, u32[]{:S(2)}, u32[]{:S(2)}) collective-permute-start(bf16[2097152]{0:T(1024)(128)(2,1)} %reduce), channel_id=1, source_target_pairs={{0,4},{4,0},{8,12},{12,8},{1,5},{5,1},{9,13},{13,9},{2,6},{6,2},{1... | collective-permute-start | bytes 12582920 | tf_op jit(solution)/shard_map/ppermute | solution.py:16
  204.2 17.5 %copy-start.2 = (bf16[1,128,4096]{2,1,0:T(8,128)(2,1)S(1)}, bf16[1,128,4096]{2,1,0:T(8,128)(2,1)}, u32[]{:S(2)}) copy-start(bf16[1,128,4096]{2,1,0:T(8,128)(2,1)} %param.8) | copy-start | bytes 3145732
  204.2 17.8 %copy-start.8 = (f32[1,4096]{1,0:T(1,128)S(1)}, f32[1,4096]{1,0:T(1,128)}, u32[]{:S(2)}) copy-start(f32[1,4096]{1,0:T(1,128)} %param.9) | copy-start | bytes 49156
  204.2 410.8 %collective-permute-start.1 = (bf16[4194304]{0:T(1024)(128)(2,1)}, bf16[4194304]{0:T(1024)(128)(2,1)}, u32[]{:S(2)}, u32[]{:S(2)}) collective-permute-start(bf16[4194304]{0:T(1024)(128)(2,1)} %maximum_select_fusion.1), channel_id=1, source_target_pairs={{0,8},{4,12},{8,0},{12,4},{1,9},{5,13},{9,1},{13,5},{2,10},{6,14},... | collective-permute-start | bytes 25165832 | tf_op jit(solution)/shard_map/ppermute | solution.py:16
  214.3 366.5 %copy-start.7 = (s32[1,4]{1,0:T(1,128)S(1)}, s32[1,4]{1,0:T(1,128)}, u32[]{:S(2)}) copy-start(s32[1,4]{1,0:T(1,128)} %param.14) | copy-start | bytes 52
  597.1 10.5 %copy-start = (bf16[512,4096]{1,0:T(8,128)(2,1)S(1)}, bf16[512,4096]{1,0:T(8,128)(2,1)}, u32[]{:S(2)}) copy-start(bf16[512,4096]{1,0:T(8,128)(2,1)} %concatenate.53) | copy-start | bytes 12582916
  597.1 11.7 %copy-start.1 = (bf16[512,4096]{1,0:T(8,128)(2,1)S(1)}, bf16[512,4096]{1,0:T(8,128)(2,1)}, u32[]{:S(2)}) copy-start(bf16[512,4096]{1,0:T(8,128)(2,1)} %concatenate.54) | copy-start | bytes 12582916
  653.2 50.7 %copy-start.3 = (f32[4096]{0:T(1024)S(1)}, f32[4096]{0:T(1024)}, u32[]{:S(2)}) copy-start(f32[4096]{0:T(1024)} %param.13) | copy-start | bytes 49156
  653.2 50.7 %copy-start.4 = (f32[4096]{0:T(1024)S(1)}, f32[4096]{0:T(1024)}, u32[]{:S(2)}) copy-start(f32[4096]{0:T(1024)} %param.12) | copy-start | bytes 49156
  653.2 72.1 %copy-start.5 = (s32[2]{0:T(128)S(1)}, s32[2]{0:T(128)}, u32[]{:S(2)}) copy-start(s32[2]{0:T(128)} %param.15) | copy-start | bytes 28
  700.4 25.7 %collective-permute-start.2 = (bf16[128,4096]{1,0:T(8,128)(2,1)S(1)}, bf16[128,4096]{1,0:T(8,128)(2,1)S(1)}, u32[]{:S(2)}, u32[]{:S(2)}) collective-permute-start(bf16[128,4096]{1,0:T(8,128)(2,1)S(1)} %fusion.21), channel_id=1, source_target_pairs={{0,16},{1,17},{2,18},{3,19},{4,20},{5,21},{6,22},{7,23},{8,24},{9,... | collective-permute-start | bytes 3145736 | tf_op jit(solution)/shard_map/ppermute | solution.py:27
  725.3 1.8 copy-start.6
Sparse Core Ops, SparseCore 0:
  664.4 34.4 all-reduce.2
